TPU v7x, 32 devices: a whole 2x2x4 slice. The times are simulated.
32 devices in a mesh: section: 8 (over z, x), tensor: 4 (over y, core).
Axes of the slice: x: 2, y: 2, z: 4, core: 2. Of those that a mesh axis runs over, the one named last changes fastest.
Arguments:
- layer_input: bfloat16 [1024, 8192], P('section'), may hold values from -36 to 36
- norm_gain: float32 [8192], replicated, may hold values from 0.5 to 1.5
- kv_weight: bfloat16 [8192, 2048], P('section', 'tensor'), may hold values from -0.0625 to 0.0625
- kv_cotangent: bfloat16 [1024, 2048], P('section', 'tensor'), may hold values from -4 to 4
Outputs:
- weight_grad: float32 [8192, 2048], P('section', 'tensor')
- input_grad: bfloat16 [1024, 8192], P('section')
All inputs are finite; a program needn't handle non-finite values.
Results may differ from a plain program's by a relative error of at most 0.0029.
Values may be sent and summed in bfloat16 or wider, within the bound.
A program may use at most 64 MiB of HBM per device.

v0:
```python
import jax
import jax.numpy as jnp
from jax import lax
from jax.sharding import PartitionSpec as P


def per_device(layer_input, norm_gain, kv_weight, kv_cotangent):
    hidden = layer_input.astype(jnp.float32)
    inv_rms = lax.rsqrt(jnp.mean(hidden * hidden, axis=1, keepdims=True) + 1e-05)
    unit_rows = hidden * inv_rms
    normed = (unit_rows * norm_gain).astype(jnp.bfloat16)
    width = hidden.shape[1]
    gathered = lax.all_gather(kv_weight, "section", axis=0, tiled=True)
    regrouped = lax.all_to_all(gathered, "tensor", split_axis=0, concat_axis=1, tiled=True)
    all_columns = lax.all_gather(kv_cotangent, "tensor", axis=1, tiled=True)
    share = regrouped.shape[0]
    offset = lax.axis_index("tensor") * share
    gain_share = lax.dynamic_slice_in_dim(norm_gain, offset, share, 0)
    unit_share = lax.dynamic_slice_in_dim(unit_rows, offset, share, 1)
    grad_part = lax.dot_general(
        all_columns, regrouped, (((1,), (1,)), ((), ())), preferred_element_type=jnp.float32
    )
    scaled_share = gain_share * grad_part
    along_part = jnp.sum(scaled_share * unit_share, axis=1, keepdims=True)
    along_unit = lax.psum(along_part, "tensor") / width
    share_grad = (inv_rms * (scaled_share - unit_share * along_unit)).astype(jnp.bfloat16)
    input_grad = lax.all_gather(share_grad, "tensor", axis=1, tiled=True)
    slabs = lax.all_to_all(normed, "section", split_axis=1, concat_axis=0, tiled=True)
    weight_grad = lax.dot_general(
        slabs,
        lax.all_gather(kv_cotangent, "section", axis=0, tiled=True),
        (((0,), (0,)), ((), ())),
        preferred_element_type=jnp.float32,
    )
    return (weight_grad, input_grad)


def solution(mesh):
    return jax.shard_map(
        per_device,
        mesh=mesh,
        in_specs=(P("section", None), P(), P("section", "tensor"), P("section", "tensor")),
        out_specs=(P("section", "tensor"), P("section", None)),
        check_vma=False,
    )
```

profile of v0, /device:TPU:1, one launch (start us, length us, event | category | flops | bytes accessed | tf_op | source)
XLA Modules:
  0.0 306.3 jit_solution(18058920644336088521)
XLA Ops:
  7.2 0.0 all-gather.6.cloned.1.call-start
  7.2 0.7 all-gather.6.cloned.1.call-update
  7.9 128.1 %all-gather.6.cloned.1.call-done = bf16[8192,512]{1,0:T(8,128)(2,1)} async-done(((bf16[1024,512]{1,0:T(8,128)(2,1)}), bf16[8192,512]{1,0:T(8,128)(2,1)}) %all-gather.6.cloned.1.call-update) | async-done | bytes 8388624 | tf_op jit(solution)/shard_map/all_gather | solution.py:13
  136.0 0.0 copy-start
  136.0 0.0 copy-start.2
  136.0 7.1 %all-to-all-start.1 = ((bf16[4,2048,512]{2,1,0:T(8,128)(2,1)}), bf16[4,2048,512]{2,1,0:T(8,128)(2,1)}, u32[]{:S(2)}, u32[]{:S(2)}) async-start(bf16[4,2048,512]{2,1,0:T(8,128)(2,1)} %bitcast.18), calls=%async_computation.1 | async-start | bytes 16777216 | tf_op jit(solution)/shard_map/all_to_all | solution.py:14
  143.1 0.0 all-gather.4.cloned.1.call-start
  143.1 0.7 all-gather.4.cloned.1.call-update
  143.8 0.0 copy-done
  143.8 0.5 fusion
  144.3 0.0 copy-done.2
  144.3 3.4 %convert_multiply_fusion = (f32[128,8192]{1,0:T(8,128)}, bf16[128,8192]{1,0:T(8,128)(2,1)}) fusion(bf16[128,8192]{1,0:T(8,128)(2,1)S(1)} %copy-done, f32[128]{0:T(128)S(1)} %add_rsqrt_fusion, f32[8192]{0:T(1024)S(1)} %copy-done.2), kind=kLoop, calls=%fused_computation | loop fusion | flops 4194304 | bytes 8421888 | tf_op jit(solution)/shard_map/mul | solution.py:10
  147.7 0.0 copy-start.1
  147.7 3.2 %copy.11 = bf16[16,8,8,1024]{3,2,0,1:T(8,128)(2,1)} copy(bf16[16,8,8,1024]{3,2,1,0:T(8,128)(2,1)} %bitcast.19) | data formatting | bytes 4194304 | tf_op jit(solution)/shard_map/all_to_all | solution.py:28
  150.9 0.0 copy-done.1
  150.9 88.7 %all_gather.13 = bf16[128,2048]{1,0:T(8,128)(2,1)S(1)} all-gather(bf16[128,512]{1,0:T(8,128)(2,1)S(1)} %copy-done.1), channel_id=1, replica_groups=mesh['section'=8,'tensor'=4] {'tensor'}, dimensions={1}, use_global_device_ids=true | all-gather | bytes 655360 | tf_op jit(solution)/shard_map/all_gather | solution.py:15
  239.7 0.0 all-to-all-done.1
  239.7 4.4 %all-to-all-start = ((bf16[128,8,1024]{2,0,1:T(8,128)(2,1)}), bf16[128,8,1024]{2,0,1:T(8,128)(2,1)}, u32[]{:S(2)}, u32[]{:S(2)}) async-start(bf16[128,8,1024]{2,0,1:T(8,128)(2,1)} %bitcast.16), calls=%async_computation | async-start | bytes 4194304 | tf_op jit(solution)/shard_map/all_to_all | solution.py:28
  244.0 0.0 all-gather.8.cloned.1.call-start
  244.1 0.0 dynamic-slice-start
  244.1 11.5 %copy.8 = bf16[2048,4,512]{0,2,1:T(8,128)(2,1)} copy(bf16[2048,4,512]{2,0,1:T(8,128)(2,1)} %bitcast.3) | data formatting | bytes 16777216 | tf_op jit(solution)/shard_map/all_to_all | solution.py:14
  255.6 0.0 dynamic-slice-done
  255.6 5.0 %multiply_reduce_fusion = (f32[128]{0:T(128)S(1)}, f32[128,2048]{1,0:T(8,128)S(1)}) fusion(f32[128,8192]{1,0:T(8,128)} %get-tuple-element.2, s32[]{:T(128)} %select_n.4, bf16[128,2048]{1,0:T(8,128)(2,1)S(1)} %all_gather.13, bf16[2048,2048]{0,1:T(8,128)(2,1)} %bitcast.17, f32[2048]{0:T(1024)S(1)} %dynamic-slice-done), kind=kOutput, calls=%fused_computation.7 | convolution fusion | flops 1074528128 | bytes 11018756 | tf_op jit(solution)/shard_map/dot_general | solution.py:20
  260.5 5.5 %psum.7 = f32[128,1]{0,1:T(1,128)S(1)} all-reduce(f32[128,1]{0,1:T(1,128)S(1)} %bitcast.20), channel_id=1, replica_groups=mesh['section'=8,'tensor'=4] {'tensor'}, use_global_device_ids=true, to_apply=%region_2.0 | all-reduce | flops 128 | bytes 1024 | tf_op jit(solution)/shard_map/psum | solution.py:25
  266.1 2.3 multiply_convert_fusion.1
  268.3 0.0 all-gather.8.cloned.1.call-update
  268.4 0.0 all-gather.4.cloned.1.call-done
  268.4 23.8 %all-to-all-done = bf16[128,8,1024]{2,0,1:T(8,128)(2,1)} async-done(((bf16[128,8,1024]{2,0,1:T(8,128)(2,1)}), bf16[128,8,1024]{2,0,1:T(8,128)(2,1)}, u32[]{:S(2)}, u32[]{:S(2)}) %all-to-all-start) | async-done | bytes 2097184 | tf_op jit(solution)/shard_map/all_to_all | solution.py:28
  292.2 4.5 %fusion.1 = f32[1024,512]{1,0:T(8,128)} fusion(bf16[1024,1024]{1,0:T(8,128)(2,1)} %bitcast.1, bf16[1024,512]{1,0:T(8,128)(2,1)} %all-gather.4.cloned.1.call-done), kind=kOutput, calls=%fused_computation.10 | convolution fusion | flops 1073741824 | bytes 5242880 | tf_op jit(solution)/shard_map/dot_general | solution.py:29
  296.6 0.0 all-gather.8.cloned.1.call-done
  296.6 3.1 %copy.13 = bf16[128,8192]{1,0:T(8,128)(2,1)} copy(bf16[128,8192]{1,0:T(8,128)(2,1)} %all-gather.8.cloned.1.call-done) | data formatting | bytes 4194304
  (2 shorter events, 0.0 us)
Async XLA Ops:
  7.2 128.8 %all-gather.6.cloned.1.call-start = ((), (), s32[]{:S(2)}) async-start(), calls=%async_computation.3 | async-start | bytes 9437184 | tf_op jit(solution)/shard_map/all_gather | solution.py:13
  136.0 7.8 %copy-start = (bf16[128,8192]{1,0:T(8,128)(2,1)S(1)}, bf16[128,8192]{1,0:T(8,128)(2,1)}, u32[]{:S(2)}) copy-start(bf16[128,8192]{1,0:T(8,128)(2,1)} %param.4) | copy-start | bytes 6291460
  136.0 8.4 %copy-start.2 = (f32[8192]{0:T(1024)S(1)}, f32[8192]{0:T(1024)}, u32[]{:S(2)}) copy-start(f32[8192]{0:T(1024)} %param.5) | copy-start | bytes 98308
  136.0 103.7 %all-to-all-start.1 = ((bf16[4,2048,512]{2,1,0:T(8,128)(2,1)}), bf16[4,2048,512]{2,1,0:T(8,128)(2,1)}, u32[]{:S(2)}, u32[]{:S(2)}) async-start(bf16[4,2048,512]{2,1,0:T(8,128)(2,1)} %bitcast.18), calls=%async_computation.1 | async-start | bytes 16777216 | tf_op jit(solution)/shard_map/all_to_all | solution.py:14
  143.1 125.3 %all-gather.4.cloned.1.call-start = ((), (), s32[]{:S(2)}) async-start(), calls=%async_computation.2 | async-start | bytes 1179648 | tf_op jit(solution)/shard_map/all_gather | solution.py:31
  147.7 3.2 %copy-start.1 = (bf16[128,512]{1,0:T(8,128)(2,1)S(1)}, bf16[128,512]{1,0:T(8,128)(2,1)}, u32[]{:S(2)}) copy-start(bf16[128,512]{1,0:T(8,128)(2,1)} %param.7) | copy-start | bytes 393220
  239.7 52.5 %all-to-all-start = ((bf16[128,8,1024]{2,0,1:T(8,128)(2,1)}), bf16[128,8,1024]{2,0,1:T(8,128)(2,1)}, u32[]{:S(2)}, u32[]{:S(2)}) async-start(bf16[128,8,1024]{2,0,1:T(8,128)(2,1)} %bitcast.16), calls=%async_computation | async-start | bytes 4194304 | tf_op jit(solution)/shard_map/all_to_all | solution.py:28
  244.0 52.6 %all-gather.8.cloned.1.call-start = ((), (), s32[]{:S(2)}) async-start(), calls=%async_computation.4 | async-start | bytes 2621440 | tf_op jit(solution)/shard_map/all_gather | solution.py:27
  244.1 11.5 %dynamic-slice-start = ((f32[8192]{0:T(1024)}, s32[]{:T(128)}), f32[2048]{0:T(1024)S(1)}, s32[]{:S(2)}) async-start(f32[8192]{0:T(1024)} %param.5, s32[]{:T(128)} %select_n.4), calls=%async_computation.5 | async-start | bytes 16896 | tf_op jit(solution)/shard_map/dynamic_slice | solution.py:18
Sparse Core Ops, SparseCore 0:
  10.1 125.8 all-gather.5
  146.0 36.6 all-gather.3
  268.5 24.4 all-gather.7
where the time goes:
time: 308 us; the launch traced here: 306 us
  waiting for transfers between devices  153 us (50%)
  blocking collectives  94.3 us (31%)
  local copies, waits for them, and re-layouts  17.8 us (6%)
  between operations  13.8 us (4%)
  starting transfers between devices  11.5 us (4%)
  matrix products  9.44 us (3%)
  other arithmetic  6.18 us (2%)
    all_gather x1, waiting for transfers between devices, per_device(): gathered = lax.all_gather(kv_weight, 'section', axis=0, tiled=True)  128 us
    all_gather x1, blocking collectives, per_device(): all_columns = lax.all_gather(kv_cotangent, 'tensor', axis=1, tiled=True)  88.7 us
    all_to_all x1, waiting for transfers between devices, per_device(): lax.all_to_all(normed, 'section', split_axis=1, concat_axis=0, tiled=True)  23.8 us
    all_to_all x1, local copies, waits for them, and re-layouts, per_device(): lax.all_to_all(gathered, 'tensor', split_axis=0, concat_axis=1, tiled=True)  11.5 us
    all_to_all x1, starting transfers between devices, per_device(): lax.all_to_all(gathered, 'tensor', split_axis=0, concat_axis=1, tiled=True)  7.11 us
  transfers between devices with their start and end apart: 5, of which 2 were waited for; matrix products, arithmetic and copies ran while one was open for 10% of the time, Pallas kernels for 0%

commit v1 on v0

v1 whole, which is shorter than its diff:
```python
import jax
import jax.numpy as jnp
from jax import lax
from jax.sharding import PartitionSpec as P


def per_device(layer_input, norm_gain, kv_weight, kv_cotangent):
    hidden = layer_input.astype(jnp.float32)
    width = hidden.shape[1]
    inv_own = lax.rsqrt(jnp.mean(hidden * hidden, axis=1, keepdims=True) + 1e-05)
    slab = lax.all_to_all(layer_input, "section", split_axis=1, concat_axis=0, tiled=True)
    cotangents = lax.all_gather(kv_cotangent, "section", axis=0, tiled=True)
    inv_rms = lax.all_gather(inv_own, "section", axis=0, tiled=True)
    rows, columns = slab.shape
    tensors = lax.axis_size("tensor")
    share = columns // tensors
    start = lax.axis_index("section") * columns
    gain = lax.dynamic_slice_in_dim(norm_gain, start, columns, 0)
    unit = slab.astype(jnp.float32) * inv_rms
    scaled_unit = unit * gain
    part = lax.dot_general(
        cotangents, kv_weight, (((1,), (1,)), ((), ())), preferred_element_type=jnp.float32
    )
    along = lax.psum(jnp.sum(part * scaled_unit, axis=1, keepdims=True), ("section", "tensor")) / width
    weight_grad = lax.dot_general(
        scaled_unit.astype(jnp.bfloat16),
        cotangents,
        (((0,), (0,)), ((), ())),
        preferred_element_type=jnp.float32,
    )
    reduced = lax.psum_scatter(part, "tensor", scatter_dimension=1, tiled=True)
    offset = lax.axis_index("tensor") * share
    gain_share = lax.dynamic_slice_in_dim(gain, offset, share, 0)
    unit_share = lax.dynamic_slice_in_dim(unit, offset, share, 1)
    share_grad = (inv_rms * (gain_share * reduced - unit_share * along)).astype(jnp.bfloat16)
    mine = lax.all_to_all(share_grad, "section", split_axis=0, concat_axis=0, tiled=True)
    sections = lax.axis_size("section")
    tokens = rows // sections
    every = lax.all_gather(mine, "tensor", axis=0, tiled=False)
    every = every.reshape(tensors, sections, tokens, share)
    input_grad = every.transpose(2, 1, 0, 3).reshape(tokens, width)
    return (weight_grad, input_grad)


def solution(mesh):
    return jax.shard_map(
        per_device,
        mesh=mesh,
        in_specs=(P("section", None), P(), P("section", "tensor"), P("section", "tensor")),
        out_specs=(P("section", "tensor"), P("section", None)),
        check_vma=False,
    )
```

time: 308 us -> 194 us (0.63)
  waiting for transfers between devices: 153 us -> 32.9 us
  blocking collectives: 94.3 us -> 113 us
  local copies, waits for them, and re-layouts: 17.8 us -> 12.6 us
  starting transfers between devices: 11.5 us -> 6.46 us
    all_gather x3 -> x2, waiting for transfers between devices: 128 us -> 28.5 us  [the longest x1 17.5 us: per_device(): every = lax.all_gather(mine, 'tensor', axis=0, tiled=False)]
    psum x1, blocking collectives: 5.52 us -> 47.7 us  [per_device(): lax.psum(jnp.sum(part * scaled_unit, axis=1, keepdims=True), ('section',...]
    all_gather x1, blocking collectives: 88.7 us -> 46.8 us  [per_device(): inv_rms = lax.all_gather(inv_own, 'section', axis=0, tiled=True)]
    all_to_all x2 -> x1, waiting for transfers between devices: 23.8 us -> 0.01 us  [per_device(): lax.all_to_all(layer_input, 'section', split_axis=1, concat_axis=0, tiled...]
    all_to_all x0 -> x1, blocking collectives: none -> 18.7 us  [per_device(): lax.all_to_all(share_grad, 'section', split_axis=0, concat_axis=0, tiled=...]
    all_to_all x2 -> x1, local copies, waits for them, and re-layouts: 14.6 us -> 1.01 us  [per_device(): lax.all_to_all(share_grad, 'section', split_axis=0, concat_axis=0, tiled=...]
    all_to_all x2 -> x1, starting transfers between devices: 11.5 us -> 6.34 us  [per_device(): lax.all_to_all(layer_input, 'section', split_axis=1, concat_axis=0, tiled...]
    unnamed x7 -> x6, local copies, waits for them, and re-layouts: 3.11 us -> 7.06 us
  transfers between devices with their start and end apart: 5 -> 4, of which waited for: 2 -> 3; matrix products, arithmetic and copies ran while one was open for 10% -> 4% of each run, Pallas kernels for 0% -> 0%
where the time goes in v1:
time: 194 us; the launch traced here: 193 us
  blocking collectives  113 us (58%)
  waiting for transfers between devices  32.9 us (17%)
  between operations  13.8 us (7%)
  local copies, waits for them, and re-layouts  12.6 us (6%)
  matrix products  10.6 us (5%)
  starting transfers between devices  6.46 us (3%)
  other arithmetic  3.86 us (2%)
    psum x1, blocking collectives, per_device(): lax.psum(jnp.sum(part * scaled_unit, axis=1, keepdims=True), ('section',...  47.7 us
    all_gather x1, blocking collectives, per_device(): inv_rms = lax.all_gather(inv_own, 'section', axis=0, tiled=True)  46.8 us
    all_to_all x1, blocking collectives, per_device(): lax.all_to_all(share_grad, 'section', split_axis=0, concat_axis=0, tiled=...  18.7 us
    all_gather x1, waiting for transfers between devices, per_device(): every = lax.all_gather(mine, 'tensor', axis=0, tiled=False)  17.5 us
    all_gather x1, waiting for transfers between devices, per_device(): cotangents = lax.all_gather(kv_cotangent, 'section', axis=0, tiled=True)  11 us
    unnamed x6, local copies, waits for them, and re-layouts  7.06 us
    all_to_all x1, starting transfers between devices, per_device(): lax.all_to_all(layer_input, 'section', split_axis=1, concat_axis=0, tiled...  6.34 us
    dot_general x1, matrix products, per_device(): lax.dot_general(cotangents, kv_weight, (((1,), (1,)), ((), ())), preferre...  5.78 us
  transfers between devices with their start and end apart: 4, of which 3 were waited for; matrix products, arithmetic and copies ran while one was open for 4% of the time, Pallas kernels for 0%

profile of v1, /device:TPU:1, one launch (start us, length us, event | category | flops | bytes accessed | tf_op | source)
XLA Modules:
  0.0 193.5 jit_solution(12077289144438562020)
XLA Ops:
  7.2 0.0 copy-start
  7.2 4.2 %copy.18 = bf16[128,8192]{0,1:T(8,128)(2,1)} copy(bf16[128,8192]{1,0:T(8,128)(2,1)} %param.4) | data formatting | bytes 4194304 | tf_op args[0]
  11.3 6.3 %all-to-all-start = ((bf16[128,8,1024]{0,2,1:T(8,128)(2,1)}), bf16[128,8,1024]{0,2,1:T(8,128)(2,1)S(1)}, u32[]{:S(2)}, u32[]{:S(2)}) async-start(bf16[128,8,1024]{0,2,1:T(8,128)(2,1)} %bitcast.26), calls=%async_computation | async-start | bytes 4194304 | tf_op jit(solution)/shard_map/all_to_all | solution.py:11
  17.7 0.0 all-gather.5.cloned.1.call-start
  17.7 0.7 all-gather.5.cloned.1.call-update
  18.4 0.0 reduce-scatter.2.cloned.1.call-start
  18.5 0.7 dynamic_slice.11
  19.2 2.1 %multiply_reduce_fusion.1 = f32[128]{0:T(128)S(1)} fusion(bf16[128,8192]{1,0:T(8,128)(2,1)} %param.4), kind=kLoop, calls=%fused_computation.3 | loop fusion | flops 3145600 | bytes 2097664 | tf_op jit(solution)/shard_map/reduce_sum | solution.py:10
  21.2 46.8 %all-gather.1 = f32[8,1,128]{2,1,0:T(1,128)S(1)} all-gather(f32[1,1,128]{2,1,0:T(1,128)S(1)} %rsqrt_bitcast_fusion), channel_id=2, replica_groups=mesh['section'=8,'tensor'=4] {'section'}, dimensions={0}, use_global_device_ids=true | all-gather | bytes 4608 | tf_op jit(solution)/shard_map/all_gather | solution.py:13
  68.0 11.0 %all-gather.5.cloned.1.call-done = bf16[1024,512]{1,0:T(8,128)(2,1)} async-done(((bf16[128,512]{1,0:T(8,128)(2,1)}), bf16[1024,512]{1,0:T(8,128)(2,1)}) %all-gather.5.cloned.1.call-update) | async-done | bytes 1048592 | tf_op jit(solution)/shard_map/all_gather | solution.py:12
  79.0 0.0 all-to-all-done
  79.0 0.0 copy-done
  79.0 5.8 %multiply_reduce_fusion = (f32[1024]{0:T(1024)S(1)}, f32[1024,1024]{0,1:T(8,128)}, f32[1024,1024]{0,1:T(8,128)}) fusion(f32[1024]{0:T(1024)S(1)} %dynamic_slice.11, f32[1024]{0:T(1024)S(1)} %bitcast.30, bf16[1024,512]{1,0:T(8,128)(2,1)} %all-gather.5.cloned.1.call-done, bf16[1024,512]{1,0:T(8,128)(2,1)S(1)} %copy-done, ...), kind=kOutput, calls=%fused_computation.2 | convolution fusion | flops 1078983680 | bytes 12595200 | tf_op jit(solution)/shard_map/dot_general | solution.py:21
  84.8 0.0 copy-start.1
  84.8 0.0 reduce-scatter.2.cloned.1.call-update
  84.8 0.0 all-gather.7.cloned.1.call-start
  84.9 0.8 dynamic_slice.13
  85.7 47.7 %psum.7 = f32[1024,1]{0,1:T(1,128)S(1)} all-reduce(f32[1024,1]{0,1:T(1,128)S(1)} %bitcast.32), channel_id=1, replica_groups=mesh['section'=8,'tensor'=4] {'section','tensor'}, use_global_device_ids=true, to_apply=%region_3.0 | all-reduce | flops 1024 | bytes 8192 | tf_op jit(solution)/shard_map/psum | solution.py:24
  133.4 3.8 %reduce-scatter.2.cloned.1.call-done = f32[1024,256]{0,1:T(8,128)} async-done(((f32[1024,1024]{0,1:T(8,128)}), f32[1024,256]{0,1:T(8,128)}) %reduce-scatter.2.cloned.1.call-update) | async-done | bytes 1048592 | tf_op jit(solution)/shard_map/reduce_scatter | solution.py:31
  137.2 1.8 copy_bitcast_fusion
  139.0 18.7 %all_to_all.22 = bf16[8,128,256]{1,2,0:T(8,128)(2,1)S(1)} all-to-all(bf16[8,128,256]{1,2,0:T(8,128)(2,1)S(1)} %copy_bitcast_fusion), channel_id=1, replica_groups=mesh['section'=8,'tensor'=4] {'section'}, dimensions={0} | all-to-all | bytes 1048576 | tf_op jit(solution)/shard_map/all_to_all | solution.py:36
  157.7 1.0 copy.21
  158.7 0.0 all-gather.7.cloned.1.call-update
  158.7 0.0 copy-done.1
  158.7 4.8 %fusion = f32[1024,512]{1,0:T(8,128)} fusion(bf16[1024,512]{1,0:T(8,128)(2,1)S(1)} %copy-done.1, f32[1024,1024]{0,1:T(8,128)} %get-tuple-element.9, f32[1024]{0:T(1024)S(1)} %dynamic_slice.11), kind=kOutput, calls=%fused_computation.5 | convolution fusion | flops 1075838976 | bytes 7344128 | tf_op jit(solution)/shard_map/dot_general | solution.py:25
  163.5 17.5 %all-gather.7.cloned.1.call-done = bf16[4,1024,256]{2,1,0:T(8,128)(2,1)} async-done(((bf16[1,1024,256]{2,1,0:T(8,128)(2,1)}), bf16[4,1024,256]{2,1,0:T(8,128)(2,1)}) %all-gather.7.cloned.1.call-update) | async-done | bytes 2097168 | tf_op jit(solution)/shard_map/all_gather | solution.py:39
  181.0 3.0 %copy.22 = bf16[128,8,4,256]{0,3,2,1:T(8,128)(2,1)S(1)} copy(bf16[128,8,4,256]{3,0,1,2:T(8,128)(2,1)} %bitcast.28) | data formatting | bytes 4194304 | tf_op jit(solution)/shard_map/transpose | solution.py:41
  184.1 2.9 %copy.23 = bf16[128,8192]{1,0:T(8,128)(2,1)} copy(bf16[128,8192]{0,1:T(8,128)(2,1)S(1)} %bitcast.27) | data formatting | bytes 4194304
  (2 shorter events, 0.0 us)
Async XLA Ops:
  7.2 71.8 %copy-start = (bf16[1024,512]{1,0:T(8,128)(2,1)S(1)}, bf16[1024,512]{1,0:T(8,128)(2,1)}, u32[]{:S(2)}) copy-start(bf16[1024,512]{1,0:T(8,128)(2,1)} %param.6) | copy-start | bytes 3145732
  11.3 67.7 %all-to-all-start = ((bf16[128,8,1024]{0,2,1:T(8,128)(2,1)}), bf16[128,8,1024]{0,2,1:T(8,128)(2,1)S(1)}, u32[]{:S(2)}, u32[]{:S(2)}) async-start(bf16[128,8,1024]{0,2,1:T(8,128)(2,1)} %bitcast.26), calls=%async_computation | async-start | bytes 4194304 | tf_op jit(solution)/shard_map/all_to_all | solution.py:11
  17.7 61.3 %all-gather.5.cloned.1.call-start = ((), (), s32[]{:S(2)}) async-start(), calls=%async_computation.3 | async-start | bytes 1179648 | tf_op jit(solution)/shard_map/all_gather | solution.py:12
  18.4 118.8 %reduce-scatter.2.cloned.1.call-start = ((), (), s32[]{:S(2)}) async-start(), calls=%async_computation.4 | async-start | bytes 5242880 | tf_op jit(solution)/shard_map/reduce_scatter | solution.py:31
  84.8 73.9 %copy-start.1 = (bf16[1024,512]{1,0:T(8,128)(2,1)S(1)}, bf16[1024,512]{1,0:T(8,128)(2,1)}, u32[]{:S(2)}) copy-start(bf16[1024,512]{1,0:T(8,128)(2,1)} %all-gather.5.cloned.1.call-done) | copy-start | bytes 3145732
  84.8 96.2 %all-gather.7.cloned.1.call-start = ((), (), s32[]{:S(2)}) async-start(), calls=%async_computation.5 | async-start | bytes 2621440 | tf_op jit(solution)/shard_map/all_gather | solution.py:39
Sparse Core Ops, SparseCore 0:
  20.6 58.3 all-gather.4
  84.9 52.2 reduce-scatter.1
  158.8 22.1 all-gather.6

commit v2 on v0

v2 whole, which is shorter than its diff:
```python
import functools

import jax
import jax.numpy as jnp
from jax import lax
from jax.experimental import pallas as pl
from jax.experimental.pallas import tpu as pltpu
from jax.sharding import PartitionSpec as P

MESH = pl.DeviceIdType.MESH
F32 = jnp.float32
BF16 = jnp.bfloat16
NT = (((1,), (1,)), ((), ()))
TN = (((0,), (0,)), ((), ()))


def kernel(S, T, x, gain, w, dyin, wg, out, invs, invcol, colbuf, dy, dym, wm, xo, xm, nrm, part,
           prcv, albuf, agbuf, alf, fin, inv_s, inv_r, dy_s, dy_r, dm_s, dm_r, wm_s, wm_r, x_s, x_r,
           xm_s, xm_r, p_s, p_r, al_s, al_r, ag_s, ag_r, o_s, o_r, oy_s, oy_r, oc_s, oc_r):
    s = lax.axis_index("section")
    t = lax.axis_index("tensor")
    c = t % 2
    g = t // 2
    G = T // 2
    mate = g * 2 + 1 - c
    tok, width = x.shape
    feats = w.shape[0]
    hf = feats // 2
    R = tok // G

    def copy(src, dst, ss, rs, sec, ten):
        return pltpu.make_async_remote_copy(
            src_ref=src, dst_ref=dst, send_sem=ss, recv_sem=rs,
            device_id={"section": sec, "tensor": ten}, device_id_type=MESH,
        )

    def loop(lo, hi, f):
        def body(k, carry):
            f(k)
            return carry
        lax.fori_loop(lo, hi, body, 0)

    def peer(k):
        return (s + k) % S

    def source(k):
        return (s + S - k) % S

    def other(d):
        return (g + d) % G

    def origin(d):
        return (g + G - d) % G

    def fcols(sec, half):
        return pl.ds(pl.multiple_of(sec * feats + half * hf, hf), hf)

    def rows(gg):
        return pl.ds(pl.multiple_of(gg * R, R), R)

    barrier = pltpu.get_barrier_semaphore()

    def hello(sec, ten):
        pl.semaphore_signal(barrier, inc=1, device_id={"section": sec, "tensor": ten}, device_id_type=MESH)

    def greet(k):
        hello(peer(k), t)
        hello(peer(k), mate)
    loop(1, S, greet)
    hello(s, mate)
    loop(1, G, lambda d: hello(s, other(d) * 2 + c))

    def squares(i, acc):
        v = x[:, pl.ds(pl.multiple_of(i * feats, feats), feats)].astype(F32)
        return acc + jnp.sum(v * v, axis=1, keepdims=True)
    total = lax.fori_loop(0, width // feats, squares, jnp.zeros((tok, 1), F32))
    inv_own = lax.rsqrt(total / width + 1e-05)
    invs[s] = jnp.transpose(jnp.broadcast_to(inv_own, (tok, 128)))[0:8]
    pl.semaphore_wait(barrier, 2 * S - 1 + G - 1)

    def wm_copy():
        half = pl.ds(pl.multiple_of((1 - c) * hf, hf), hf)
        return copy(w.at[half], wm, wm_s.at[0], wm_r.at[0], s, mate)

    def dy_copy(k):
        return copy(dyin, dy.at[s], dy_s.at[k], dy_r.at[k], peer(k), t)

    def inv_copy(k):
        return copy(invs.at[s], invs.at[s], inv_s.at[k], inv_r.at[k], peer(k), t)

    def x_copy(k):
        return copy(x.at[:, fcols(peer(k), c)], xo.at[s], x_s.at[k], x_r.at[k], peer(k), t)

    def dm_copy(k):
        return copy(dy.at[source(k)], dym.at[source(k)], dm_s.at[k], dm_r.at[k], s, mate)

    def dm_own():
        return copy(dyin, dym.at[s], dm_s.at[0], dm_r.at[0], s, mate)

    def xm_copy(k):
        return copy(xo.at[source(k)], xm.at[source(k)], xm_s.at[k], xm_r.at[k], s, mate)

    wm_copy().start()
    dm_own().start()
    loop(1, S, lambda k: dy_copy(k).start())
    loop(1, S, lambda k: inv_copy(k).start())
    loop(1, S, lambda k: x_copy(k).start())
    dy[s] = dyin[...]
    xo[s] = x[:, fcols(s, c)]
    xm[s] = x[:, fcols(s, 1 - c)]

    wm_copy().wait_recv()
    own_half = pl.ds(pl.multiple_of(c * hf, hf), hf)

    def p_copy(k, d):
        sec = source(k)
        i = k * G + d
        return copy(part.at[sec, rows(other(d))], prcv.at[d, sec], p_s.at[i], p_r.at[i], s, other(d) * 2 + c)

    def multiply(k):
        sec = source(k)
        dm_copy(k).wait_recv()
        part[sec] = lax.dot_general(dy[sec], w[own_half, :], NT, preferred_element_type=F32) + lax.dot_general(
            dym[sec], wm[...], NT, preferred_element_type=F32)

    def pass_cotangent(k):
        copy(dyin, dy.at[source(k)], dy_s.at[k], dy_r.at[k], peer(k), t).wait_recv()
        dm_copy(k).start()

    def send_part(k):
        loop(1, G, lambda d: p_copy(k, d).start())

    def stage(k):
        pass_cotangent(k)
        multiply(k - 1)
        send_part(k - 1)
    loop(1, S, stage)
    multiply(S - 1)
    send_part(S - 1)

    lanes = lax.broadcasted_iota(jnp.int32, (S, tok), 0)

    def unit_block(k, acc):
        sec = source(k)
        col = jnp.transpose(jnp.broadcast_to(invs[sec][0:1], (128, tok)))
        invcol[sec] = col
        unit = xo[sec].astype(F32) * col[:, 0:1]
        scaled = unit * gain[:, fcols(s, c)]
        nrm[pl.ds(pl.multiple_of(sec * tok, tok), tok), :] = scaled.astype(BF16)
        sums = jnp.sum(scaled * part[sec], axis=1, keepdims=True)
        row = jnp.transpose(jnp.broadcast_to(sums, (tok, 128)))[0:1]
        return jnp.where(lanes == sec, jnp.broadcast_to(row, (S, tok)), acc)

    def token_block(k, acc):
        sec = source(k)
        copy(invs.at[s], invs.at[sec], inv_s.at[k], inv_r.at[k], peer(k), t).wait_recv()
        copy(xo.at[s], xo.at[sec], x_s.at[k], x_r.at[k], peer(k), t).wait_recv()
        xm_copy(k).start()
        return unit_block(k, acc)
    along = unit_block(0, jnp.zeros((S, tok), F32))
    along = lax.fori_loop(1, S, token_block, along)
    albuf[0, 0] = along

    def al_copy(k, m):
        return copy(albuf.at[0, 0], albuf.at[k, m], al_s.at[k * 2 + m], al_r.at[k * 2 + m], peer(k),
                    t if m == 0 else mate)

    def al_send(k):
        al_copy(k, 0).start()
        al_copy(k, 1).start()
    al_copy(0, 1).start()
    loop(1, S, al_send)

    def weight_half(half):
        flat = dy[...].reshape(S * tok, dyin.shape[1])
        wg[pl.ds(pl.multiple_of(half * hf, hf), hf), :] = lax.dot_general(
            nrm[...], flat, TN, preferred_element_type=F32)
    weight_half(c)

    al_copy(0, 1).wait_recv()

    def al_wait(k, acc):
        al_copy(k, 0).wait_recv()
        al_copy(k, 1).wait_recv()
        return acc + (albuf[k, 0] + albuf[k, 1])
    along = lax.fori_loop(1, S, al_wait, albuf[0, 0] + albuf[0, 1])
    agbuf[0] = along

    def ag_copy(d):
        return copy(agbuf.at[0], agbuf.at[d], ag_s.at[d], ag_r.at[d], s, other(d) * 2 + c)
    loop(1, G, lambda d: ag_copy(d).start())

    def ag_wait(d, acc):
        ag_copy(d).wait_recv()
        return acc + agbuf[d]

    def p_wait(k):
        loop(1, G, lambda d: p_copy(k, d).wait_recv())
    loop(0, S, p_wait)
    alf[...] = lax.fori_loop(1, G, ag_wait, along) / width

    def finish(sec):
        def add(d, acc):
            return acc + prcv[d, sec]
        reduced = lax.fori_loop(1, G, add, part[sec, rows(g), :])
        colbuf[...] = jnp.transpose(jnp.broadcast_to(alf[pl.ds(sec, 1), :], (128, tok)))
        inv = invcol[sec, rows(g), :][:, 0:1]
        al = colbuf[rows(g), :][:, 0:1]
        unit = xo[sec, rows(g), :].astype(F32) * inv
        return (inv * (gain[:, fcols(s, c)] * reduced - unit * al)).astype(BF16)

    def region(sec, gg, half):
        return out.at[rows(gg), fcols(sec, half)]

    def o_copy(k):
        return copy(fin.at[peer(k)], region(s, g, c), o_s.at[k], o_r.at[k], peer(k), t)

    def oy_copy(k, d):
        place = region(source(k), g, c)
        return copy(place, place, oy_s.at[k * G + d], oy_r.at[k * G + d], s, other(d) * 2 + c)

    def oc_copy(k, d):
        place = region(source(k), origin(d), c)
        return copy(place, place, oc_s.at[k * G + d], oc_r.at[k * G + d], s, mate)

    def send_on(k):
        loop(1, G, lambda d: oy_copy(k, d).start())
        oc_copy(k, 0).start()

    def send_rows(k):
        fin[peer(k)] = finish(peer(k))
        o_copy(k).start()
    loop(1, S, send_rows)
    out[rows(g), fcols(s, c)] = finish(s)
    send_on(0)

    def mate_block(k):
        sec = source(k)
        unit = xm[sec].astype(F32) * invcol[sec][:, 0:1]
        scaled = unit * gain[:, fcols(s, 1 - c)]
        nrm[pl.ds(pl.multiple_of(sec * tok, tok), tok), :] = scaled.astype(BF16)

    def mate_wait(k):
        xm_copy(k).wait_recv()
        mate_block(k)
    mate_block(0)
    loop(1, S, mate_wait)
    weight_half(1 - c)

    def arrive(k):
        place = region(source(k), g, c)
        copy(place, place, o_s.at[k], o_r.at[k], peer(k), t).wait_recv()
        send_on(k)
    loop(1, S, arrive)

    def arrive_y(k):
        def one(d):
            place = region(source(k), origin(d), c)
            copy(place, place, oy_s.at[k * G + d], oy_r.at[k * G + d], s, mate).wait_recv()
            oc_copy(k, d).start()
        loop(1, G, one)
    loop(0, S, arrive_y)

    def arrive_mate(k):
        def one(d):
            place = region(source(k), origin(d), 1 - c)
            copy(place, place, oc_s.at[k * G + d], oc_r.at[k * G + d], s, mate).wait_recv()
        loop(0, G, one)
    loop(0, S, arrive_mate)

    wm_copy().wait_send()
    dm_own().wait_send()
    al_copy(0, 1).wait_send()
    loop(1, G, lambda d: ag_copy(d).wait_send())

    def drain(k):
        dy_copy(k).wait_send()
        inv_copy(k).wait_send()
        x_copy(k).wait_send()
        dm_copy(k).wait_send()
        xm_copy(k).wait_send()
        al_copy(k, 0).wait_send()
        al_copy(k, 1).wait_send()
        o_copy(k).wait_send()
    loop(1, S, drain)

    def drain_all(k):
        def one(d):
            p_copy(k, d).wait_send()
            oy_copy(k, d).wait_send()
            oc_copy(k, d).wait_send()
        loop(1, G, one)
        oc_copy(k, 0).wait_send()
    loop(0, S, drain_all)


def solution(mesh):
    S, T = mesh.shape["section"], mesh.shape["tensor"]
    G = T // 2

    def per_device(layer_input, norm_gain, kv_weight, kv_cotangent):
        tok, width = layer_input.shape
        feats, cols = kv_weight.shape
        hf, R = feats // 2, tok // G
        dma = pltpu.SemaphoreType.DMA
        vmem = pl.BlockSpec(memory_space=pltpu.VMEM)
        V = pltpu.VMEM
        return tuple(pl.pallas_call(
            functools.partial(kernel, S, T),
            out_shape=(jax.ShapeDtypeStruct((feats, cols), F32), jax.ShapeDtypeStruct((tok, width), BF16)),
            in_specs=[vmem] * 4,
            out_specs=(vmem, vmem),
            scratch_shapes=[
                V((S, 8, tok), F32), V((S, tok, 128), F32), V((tok, 128), F32),
                V((S, tok, cols), BF16), V((S, tok, cols), BF16), V((hf, cols), BF16),
                V((S, tok, hf), BF16), V((S, tok, hf), BF16), V((S * tok, hf), BF16),
                V((S, tok, hf), F32), V((G, S, R, hf), F32),
                V((S, 2, S, tok), F32), V((G, S, tok), F32), V((S, tok), F32), V((S, R, hf), BF16),
                dma((S,)), dma((S,)), dma((S,)), dma((S,)), dma((S,)), dma((S,)), dma((1,)), dma((1,)),
                dma((S,)), dma((S,)), dma((S,)), dma((S,)), dma((S * G,)), dma((S * G,)),
                dma((S * 2,)), dma((S * 2,)), dma((G,)), dma((G,)), dma((S,)), dma((S,)),
                dma((S * G,)), dma((S * G,)), dma((S * G,)), dma((S * G,)),
            ],
            compiler_params=pltpu.CompilerParams(
                collective_id=0, has_side_effects=True, vmem_limit_bytes=56 * 1024 * 1024),
        )(layer_input, norm_gain.reshape(1, width), kv_weight, kv_cotangent))

    return jax.shard_map(
        per_device,
        mesh=mesh,
        in_specs=(P("section", None), P(), P("section", "tensor"), P("section", "tensor")),
        out_specs=(P("section", "tensor"), P("section", None)),
        check_vma=False,
    )
```

time: 308 us -> 90.6 us (0.29)
  waiting for transfers between devices: 153 us -> 0 us
  blocking collectives: 94.3 us -> 0 us
  Pallas kernels: 0 us -> 85.3 us
  local copies, waits for them, and re-layouts: 17.8 us -> 4.55 us
  between operations: 13.8 us -> 0.65 us
  starting transfers between devices: 11.5 us -> 0 us
  matrix products: 9.44 us -> 0 us
  other arithmetic: 6.18 us -> 0 us
    all_gather x3 -> x0, waiting for transfers between devices: 128 us -> none  [the longest x1 128 us: per_device(): gathered = lax.all_gather(kv_weight, 'section', axis=0, tiled=True)]
    all_gather x1 -> x0, blocking collectives: 88.7 us -> none  [per_device(): all_columns = lax.all_gather(kv_cotangent, 'tensor', axis=1, tiled=True)]
    pallas_call x0 -> x1, Pallas kernels: none -> 85.3 us  [per_device(): pl.pallas_call(functools.partial(kernel, S, T), out_shape=(jax.ShapeDtype...]
    all_to_all x2 -> x0, waiting for transfers between devices: 23.8 us -> none  [the longest x1 23.8 us: per_device(): lax.all_to_all(normed, 'section', split_axis=1, concat_axis=0, tiled=True)]
    all_to_all x2 -> x0, local copies, waits for them, and re-layouts: 14.6 us -> none  [the longest x1 11.5 us: per_device(): lax.all_to_all(gathered, 'tensor', split_axis=0, concat_axis=1, tiled=True)]
    all_to_all x2 -> x0, starting transfers between devices: 11.5 us -> none  [the longest x1 7.11 us: per_device(): lax.all_to_all(gathered, 'tensor', split_axis=0, concat_axis=1, tiled=True)]
    dot_general x2 -> x0, matrix products: 9.44 us -> none  [the longest x1 4.98 us: per_device(): lax.dot_general(all_columns, regrouped, (((1,), (1,)), ((), ())), preferr...]
    psum x1 -> x0, blocking collectives: 5.52 us -> none  [per_device(): along_unit = lax.psum(along_part, 'tensor') / width]
  transfers between devices with their start and end apart: 5 -> 0, of which waited for: 2 -> 0; matrix products, arithmetic and copies ran while one was open for 10% -> 0% of each run, Pallas kernels for 0% -> 0%
where the time goes in v2:
time: 90.6 us; the launch traced here: 90.5 us
  Pallas kernels  85.3 us (94%)
  local copies, waits for them, and re-layouts  4.55 us (5%)
    pallas_call x1, Pallas kernels, per_device(): pl.pallas_call(functools.partial(kernel, S, T), out_shape=(jax.ShapeDtype...  85.3 us
    unnamed x4, local copies, waits for them, and re-layouts  4.55 us

profile of v2, /device:TPU:1, one launch (start us, length us, event | category | flops | bytes accessed | tf_op | source)
XLA Modules:
  0.0 90.5 jit_solution(6083792318726653427)
XLA Ops:
  0.6 85.3 %shard_map.59 = (f32[1024,512]{1,0:T(8,128)}, bf16[128,8192]{1,0:T(8,128)(2,1)}) custom-call(bf16[128,8192]{1,0:T(8,128)(2,1)} %x.1, f32[1,8192]{1,0:T(1,128)} %bitcast.1, bf16[1024,512]{1,0:T(8,128)(2,1)} %w.1, bf16[128,512]{1,0:T(8,128)(2,1)} %dyin.1), custom_call_target="tpu_custom_call" | custom-call | tf_op jit(solution)/shard_map/pallas_call | solution.py:308
  85.9 0.0 copy-start
  85.9 3.2 %copy.8 = f32[1024,512]{1,0:T(8,128)} copy(f32[1024,512]{1,0:T(8,128)} %get-tuple-element.4) | data formatting | bytes 4194304
  89.2 0.0 copy-done
  89.2 1.3 %copy.9 = bf16[128,8192]{1,0:T(8,128)(2,1)} copy(bf16[128,8192]{1,0:T(8,128)(2,1)S(1)} %copy-done) | data formatting | bytes 4194304
Async XLA Ops:
  85.9 3.2 %copy-start = (bf16[128,8192]{1,0:T(8,128)(2,1)S(1)}, bf16[128,8192]{1,0:T(8,128)(2,1)}, u32[]{:S(2)}) copy-start(bf16[128,8192]{1,0:T(8,128)(2,1)} %get-tuple-element.5) | copy-start | bytes 6291460

commit v3 on v2

--- a/solution.py
+++ b/solution.py
@@ -22,6 +22,7 @@
     c = t % 2
     g = t // 2
     G = T // 2
+    Z = S // 2
     mate = g * 2 + 1 - c
     tok, width = x.shape
     feats = w.shape[0]
@@ -41,10 +42,10 @@
         lax.fori_loop(lo, hi, body, 0)
 
     def peer(k):
-        return (s + k) % S
+        return (s // 2 + k // 2) % Z * 2 + (s + k) % 2
 
     def source(k):
-        return (s + S - k) % S
+        return (s // 2 + Z - k // 2) % Z * 2 + (s + k) % 2
 
     def other(d):
         return (g + d) % G
@@ -102,9 +103,10 @@
 
     wm_copy().start()
     dm_own().start()
-    loop(1, S, lambda k: dy_copy(k).start())
+    dy_copy(1).start()
+    loop(1, Z, lambda i: dy_copy(2 * i).start())
     loop(1, S, lambda k: inv_copy(k).start())
-    loop(1, S, lambda k: x_copy(k).start())
+    loop(1, Z, lambda i: x_copy(2 * i).start())
     dy[s] = dyin[...]
     xo[s] = x[:, fcols(s, c)]
     xm[s] = x[:, fcols(s, 1 - c)]
@@ -127,16 +129,35 @@
         copy(dyin, dy.at[source(k)], dy_s.at[k], dy_r.at[k], peer(k), t).wait_recv()
         dm_copy(k).start()
 
-    def send_part(k):
+    def relay(k):
+        return copy(dy.at[source(k)], dy.at[source(k)], dy_s.at[k + 1], dy_r.at[k + 1], peer(1), t)
+
+    def pass_relay(k):
+        pass_cotangent(k)
+        relay(k).start()
+
+    def use(k):
+        multiply(k)
         loop(1, G, lambda d: p_copy(k, d).start())
 
-    def stage(k):
-        pass_cotangent(k)
-        multiply(k - 1)
-        send_part(k - 1)
-    loop(1, S, stage)
-    multiply(S - 1)
-    send_part(S - 1)
+    pass_cotangent(1)
+    use(0)
+    pass_relay(2)
+    use(1)
+
+    def even(i):
+        pass_relay(2 * i)
+        use(2 * i - 2)
+    loop(2, Z, even)
+    loop(0, Z, lambda i: x_copy(2 * i + 1).start())
+    use(2 * Z - 2)
+    pass_cotangent(3)
+
+    def odd(i):
+        pass_cotangent(2 * i + 1)
+        use(2 * i - 1)
+    loop(2, Z, odd)
+    use(2 * Z - 1)
 
     lanes = lax.broadcasted_iota(jnp.int32, (S, tok), 0)
 
@@ -158,7 +179,8 @@
         xm_copy(k).start()
         return unit_block(k, acc)
     along = unit_block(0, jnp.zeros((S, tok), F32))
-    along = lax.fori_loop(1, S, token_block, along)
+    along = lax.fori_loop(1, Z, lambda i, acc: token_block(2 * i, acc), along)
+    along = lax.fori_loop(0, Z, lambda i, acc: token_block(2 * i + 1, acc), along)
     albuf[0, 0] = along
 
     def al_copy(k, m):
@@ -274,7 +296,6 @@
     loop(1, G, lambda d: ag_copy(d).wait_send())
 
     def drain(k):
-        dy_copy(k).wait_send()
         inv_copy(k).wait_send()
         x_copy(k).wait_send()
         dm_copy(k).wait_send()
@@ -283,6 +304,12 @@
         al_copy(k, 1).wait_send()
         o_copy(k).wait_send()
     loop(1, S, drain)
+    dy_copy(1).wait_send()
+
+    def drain_dy(i):
+        dy_copy(2 * i).wait_send()
+        relay(2 * i).wait_send()
+    loop(1, Z, drain_dy)
 
     def drain_all(k):
         def one(d):

time: 90.6 us -> 78.9 us (0.87)
  Pallas kernels: 85.3 us -> 73.5 us
    pallas_call x1, Pallas kernels: 85.3 us -> 73.5 us  [per_device(): pl.pallas_call(functools.partial(kernel, S, T), out_shape=(jax.ShapeDtype...]
where the time goes in v3:
time: 78.9 us; the launch traced here: 78.7 us
  Pallas kernels  73.5 us (93%)
  local copies, waits for them, and re-layouts  4.55 us (6%)
    pallas_call x1, Pallas kernels, per_device(): pl.pallas_call(functools.partial(kernel, S, T), out_shape=(jax.ShapeDtype...  73.5 us
    unnamed x4, local copies, waits for them, and re-layouts  4.55 us

profile of v3, /device:TPU:1, one launch (start us, length us, event | category | flops | bytes accessed | tf_op | source)
XLA Modules:
  0.0 78.7 jit_solution(4853423568661934386)
XLA Ops:
  0.6 73.5 %shard_map.59 = (f32[1024,512]{1,0:T(8,128)}, bf16[128,8192]{1,0:T(8,128)(2,1)}) custom-call(bf16[128,8192]{1,0:T(8,128)(2,1)} %x.1, f32[1,8192]{1,0:T(1,128)} %bitcast.1, bf16[1024,512]{1,0:T(8,128)(2,1)} %w.1, bf16[128,512]{1,0:T(8,128)(2,1)} %dyin.1), custom_call_target="tpu_custom_call" | custom-call | tf_op jit(solution)/shard_map/pallas_call | solution.py:335
  74.2 0.0 copy-start
  74.2 3.2 %copy.8 = f32[1024,512]{1,0:T(8,128)} copy(f32[1024,512]{1,0:T(8,128)} %get-tuple-element.4) | data formatting | bytes 4194304
  77.4 0.0 copy-done
  77.4 1.3 %copy.9 = bf16[128,8192]{1,0:T(8,128)(2,1)} copy(bf16[128,8192]{1,0:T(8,128)(2,1)S(1)} %copy-done) | data formatting | bytes 4194304
Async XLA Ops:
  74.2 3.2 %copy-start = (bf16[128,8192]{1,0:T(8,128)(2,1)S(1)}, bf16[128,8192]{1,0:T(8,128)(2,1)}, u32[]{:S(2)}) copy-start(bf16[128,8192]{1,0:T(8,128)(2,1)} %get-tuple-element.5) | copy-start | bytes 6291460

commit v4 on v3

--- a/solution.py
+++ b/solution.py
@@ -178,9 +178,36 @@
         copy(xo.at[s], xo.at[sec], x_s.at[k], x_r.at[k], peer(k), t).wait_recv()
         xm_copy(k).start()
         return unit_block(k, acc)
+
+    def grad_block(k, first=False):
+        sec = source(k)
+        if not first:
+            xm_copy(k).wait_recv()
+        unit = xm[sec].astype(F32) * invcol[sec][:, 0:1]
+        scaled = (unit * gain[:, fcols(s, 1 - c)]).astype(BF16)
+        own = nrm[pl.ds(pl.multiple_of(sec * tok, tok), tok), :]
+        for half, block in ((c, own), (1 - c, scaled)):
+            place = pl.ds(pl.multiple_of(half * hf, hf), hf)
+            term = lax.dot_general(block, dy[sec], TN, preferred_element_type=F32)
+            wg[place, :] = term if first else wg[place, :] + term
+
     along = unit_block(0, jnp.zeros((S, tok), F32))
-    along = lax.fori_loop(1, Z, lambda i, acc: token_block(2 * i, acc), along)
-    along = lax.fori_loop(0, Z, lambda i, acc: token_block(2 * i + 1, acc), along)
+    along = token_block(2, along)
+    grad_block(0, True)
+
+    def even_block(i, acc):
+        acc = token_block(2 * i, acc)
+        grad_block(2 * i - 2)
+        return acc
+
+    def odd_block(i, acc):
+        acc = token_block(2 * i + 1, acc)
+        grad_block(2 * i - 1)
+        return acc
+    along = lax.fori_loop(2, Z, even_block, along)
+    along = token_block(1, along)
+    grad_block(2 * Z - 2)
+    along = lax.fori_loop(1, Z, odd_block, along)
     albuf[0, 0] = along
 
     def al_copy(k, m):
@@ -193,11 +220,7 @@
     al_copy(0, 1).start()
     loop(1, S, al_send)
 
-    def weight_half(half):
-        flat = dy[...].reshape(S * tok, dyin.shape[1])
-        wg[pl.ds(pl.multiple_of(half * hf, hf), hf), :] = lax.dot_general(
-            nrm[...], flat, TN, preferred_element_type=F32)
-    weight_half(c)
+    grad_block(2 * Z - 1)
 
     al_copy(0, 1).wait_recv()
 
@@ -255,19 +278,6 @@
     loop(1, S, send_rows)
     out[rows(g), fcols(s, c)] = finish(s)
     send_on(0)
-
-    def mate_block(k):
-        sec = source(k)
-        unit = xm[sec].astype(F32) * invcol[sec][:, 0:1]
-        scaled = unit * gain[:, fcols(s, 1 - c)]
-        nrm[pl.ds(pl.multiple_of(sec * tok, tok), tok), :] = scaled.astype(BF16)
-
-    def mate_wait(k):
-        xm_copy(k).wait_recv()
-        mate_block(k)
-    mate_block(0)
-    loop(1, S, mate_wait)
-    weight_half(1 - c)
 
     def arrive(k):
         place = region(source(k), g, c)

time: 78.9 us -> 79.3 us (level)
  no operation moved by 1% of the time
where the time goes in v4:
time: 79.3 us; the launch traced here: 79.1 us
  Pallas kernels  73.9 us (93%)
  local copies, waits for them, and re-layouts  4.55 us (6%)
    pallas_call x1, Pallas kernels, per_device(): pl.pallas_call(functools.partial(kernel, S, T), out_shape=(jax.ShapeDtype...  73.9 us
    unnamed x4, local copies, waits for them, and re-layouts  4.55 us

profile of v4, /device:TPU:1, one launch (start us, length us, event | category | flops | bytes accessed | tf_op | source)
XLA Modules:
  0.0 79.1 jit_solution(10500848368309593233)
XLA Ops:
  0.6 73.9 %shard_map.59 = (f32[1024,512]{1,0:T(8,128)}, bf16[128,8192]{1,0:T(8,128)(2,1)}) custom-call(bf16[128,8192]{1,0:T(8,128)(2,1)} %x.1, f32[1,8192]{1,0:T(1,128)} %bitcast.1, bf16[1024,512]{1,0:T(8,128)(2,1)} %w.1, bf16[128,512]{1,0:T(8,128)(2,1)} %dyin.1), custom_call_target="tpu_custom_call" | custom-call | tf_op jit(solution)/shard_map/pallas_call | solution.py:345
  74.6 0.0 copy-start
  74.6 3.2 %copy.8 = f32[1024,512]{1,0:T(8,128)} copy(f32[1024,512]{1,0:T(8,128)} %get-tuple-element.4) | data formatting | bytes 4194304
  77.8 0.0 copy-done
  77.8 1.3 %copy.9 = bf16[128,8192]{1,0:T(8,128)(2,1)} copy(bf16[128,8192]{1,0:T(8,128)(2,1)S(1)} %copy-done) | data formatting | bytes 4194304
Async XLA Ops:
  74.6 3.2 %copy-start = (bf16[128,8192]{1,0:T(8,128)(2,1)S(1)}, bf16[128,8192]{1,0:T(8,128)(2,1)}, u32[]{:S(2)}) copy-start(bf16[128,8192]{1,0:T(8,128)(2,1)} %get-tuple-element.5) | copy-start | bytes 6291460

commit v5 on v4

--- a/solution.py
+++ b/solution.py
@@ -14,9 +14,9 @@
 TN = (((0,), (0,)), ((), ()))
 
 
-def kernel(S, T, x, gain, w, dyin, wg, out, invs, invcol, colbuf, dy, dym, wm, xo, xm, nrm, part,
-           prcv, albuf, agbuf, alf, fin, inv_s, inv_r, dy_s, dy_r, dm_s, dm_r, wm_s, wm_r, x_s, x_r,
-           xm_s, xm_r, p_s, p_r, al_s, al_r, ag_s, ag_r, o_s, o_r, oy_s, oy_r, oc_s, oc_r):
+def kernel(S, T, x_in, gain, w_in, dy_in, wg_out, out, invs, invcol, colbuf, dy, dym, wm, xo, xm, nrm, part,
+           prcv, albuf, alf, fin, x, w, dyin, wg, ld, inv_s, inv_r, dy_s, dy_r, dm_s, dm_r, wm_s, wm_r, x_s, x_r,
+           xm_s, xm_r, p_s, p_r, al_s, al_r, o_s, o_r, oy_s, oy_r, oc_s, oc_r):
     s = lax.axis_index("section")
     t = lax.axis_index("tensor")
     c = t % 2
@@ -64,12 +64,15 @@
     def hello(sec, ten):
         pl.semaphore_signal(barrier, inc=1, device_id={"section": sec, "tensor": ten}, device_id_type=MESH)
 
-    def greet(k):
-        hello(peer(k), t)
-        hello(peer(k), mate)
-    loop(1, S, greet)
-    hello(s, mate)
-    loop(1, G, lambda d: hello(s, other(d) * 2 + c))
+    def place_of(j):
+        return peer(j // T), (t + j) % T
+    loop(1, S * T, lambda j: hello(*place_of(j)))
+
+    loads = [pltpu.make_async_copy(a, b, ld.at[i])
+             for i, (a, b) in enumerate(((x_in, x), (w_in, w), (dy_in, dyin)))]
+    for load in loads:
+        load.start()
+    loads[0].wait()
 
     def squares(i, acc):
         v = x[:, pl.ds(pl.multiple_of(i * feats, feats), feats)].astype(F32)
@@ -77,7 +80,9 @@
     total = lax.fori_loop(0, width // feats, squares, jnp.zeros((tok, 1), F32))
     inv_own = lax.rsqrt(total / width + 1e-05)
     invs[s] = jnp.transpose(jnp.broadcast_to(inv_own, (tok, 128)))[0:8]
-    pl.semaphore_wait(barrier, 2 * S - 1 + G - 1)
+    loads[1].wait()
+    loads[2].wait()
+    pl.semaphore_wait(barrier, S * T - 1)
 
     def wm_copy():
         half = pl.ds(pl.multiple_of((1 - c) * hf, hf), hf)
@@ -208,41 +213,25 @@
     along = token_block(1, along)
     grad_block(2 * Z - 2)
     along = lax.fori_loop(1, Z, odd_block, along)
-    albuf[0, 0] = along
-
-    def al_copy(k, m):
-        return copy(albuf.at[0, 0], albuf.at[k, m], al_s.at[k * 2 + m], al_r.at[k * 2 + m], peer(k),
-                    t if m == 0 else mate)
-
-    def al_send(k):
-        al_copy(k, 0).start()
-        al_copy(k, 1).start()
-    al_copy(0, 1).start()
-    loop(1, S, al_send)
+    albuf[0] = along
+
+    def al_copy(j):
+        sec, ten = place_of(j)
+        return copy(albuf.at[0], albuf.at[j], al_s.at[j], al_r.at[j], sec, ten)
+    loop(1, S * T, lambda j: al_copy(j).start())
 
     grad_block(2 * Z - 1)
-
-    al_copy(0, 1).wait_recv()
-
-    def al_wait(k, acc):
-        al_copy(k, 0).wait_recv()
-        al_copy(k, 1).wait_recv()
-        return acc + (albuf[k, 0] + albuf[k, 1])
-    along = lax.fori_loop(1, S, al_wait, albuf[0, 0] + albuf[0, 1])
-    agbuf[0] = along
-
-    def ag_copy(d):
-        return copy(agbuf.at[0], agbuf.at[d], ag_s.at[d], ag_r.at[d], s, other(d) * 2 + c)
-    loop(1, G, lambda d: ag_copy(d).start())
-
-    def ag_wait(d, acc):
-        ag_copy(d).wait_recv()
-        return acc + agbuf[d]
+    store = pltpu.make_async_copy(wg, wg_out, ld.at[3])
+    store.start()
 
     def p_wait(k):
         loop(1, G, lambda d: p_copy(k, d).wait_recv())
     loop(0, S, p_wait)
-    alf[...] = lax.fori_loop(1, G, ag_wait, along) / width
+
+    def al_wait(j, acc):
+        al_copy(j).wait_recv()
+        return acc + albuf[j]
+    alf[...] = lax.fori_loop(1, S * T, al_wait, along) / width
 
     def finish(sec):
         def add(d, acc):
@@ -302,16 +291,14 @@
 
     wm_copy().wait_send()
     dm_own().wait_send()
-    al_copy(0, 1).wait_send()
-    loop(1, G, lambda d: ag_copy(d).wait_send())
+    loop(1, S * T, lambda j: al_copy(j).wait_send())
+    store.wait()
 
     def drain(k):
         inv_copy(k).wait_send()
         x_copy(k).wait_send()
         dm_copy(k).wait_send()
         xm_copy(k).wait_send()
-        al_copy(k, 0).wait_send()
-        al_copy(k, 1).wait_send()
         o_copy(k).wait_send()
     loop(1, S, drain)
     dy_copy(1).wait_send()
@@ -341,21 +328,23 @@
         hf, R = feats // 2, tok // G
         dma = pltpu.SemaphoreType.DMA
         vmem = pl.BlockSpec(memory_space=pltpu.VMEM)
+        hbm = pl.BlockSpec(memory_space=pl.ANY)
         V = pltpu.VMEM
         return tuple(pl.pallas_call(
             functools.partial(kernel, S, T),
             out_shape=(jax.ShapeDtypeStruct((feats, cols), F32), jax.ShapeDtypeStruct((tok, width), BF16)),
-            in_specs=[vmem] * 4,
-            out_specs=(vmem, vmem),
+            in_specs=[hbm, vmem, hbm, hbm],
+            out_specs=(hbm, vmem),
             scratch_shapes=[
                 V((S, 8, tok), F32), V((S, tok, 128), F32), V((tok, 128), F32),
                 V((S, tok, cols), BF16), V((S, tok, cols), BF16), V((hf, cols), BF16),
                 V((S, tok, hf), BF16), V((S, tok, hf), BF16), V((S * tok, hf), BF16),
                 V((S, tok, hf), F32), V((G, S, R, hf), F32),
-                V((S, 2, S, tok), F32), V((G, S, tok), F32), V((S, tok), F32), V((S, R, hf), BF16),
+                V((S * T, S, tok), F32), V((S, tok), F32), V((S, R, hf), BF16),
+                V((tok, width), BF16), V((feats, cols), BF16), V((tok, cols), BF16), V((feats, cols), F32), dma((4,)),
                 dma((S,)), dma((S,)), dma((S,)), dma((S,)), dma((S,)), dma((S,)), dma((1,)), dma((1,)),
                 dma((S,)), dma((S,)), dma((S,)), dma((S,)), dma((S * G,)), dma((S * G,)),
-                dma((S * 2,)), dma((S * 2,)), dma((G,)), dma((G,)), dma((S,)), dma((S,)),
+                dma((S * T,)), dma((S * T,)), dma((S,)), dma((S,)),
                 dma((S * G,)), dma((S * G,)), dma((S * G,)), dma((S * G,)),
             ],
             compiler_params=pltpu.CompilerParams(

time: 79.3 us -> 79.7 us (level)
  no operation moved by 1% of the time
where the time goes in v5:
time: 79.7 us; the launch traced here: 79.2 us
  Pallas kernels  74 us (93%)
  local copies, waits for them, and re-layouts  4.55 us (6%)
    pallas_call x1, Pallas kernels, per_device(): pl.pallas_call(functools.partial(kernel, S, T), out_shape=(jax.ShapeDtype...  74 us
    unnamed x4, local copies, waits for them, and re-layouts  4.55 us

profile of v5, /device:TPU:1, one launch (start us, length us, event | category | flops | bytes accessed | tf_op | source)
XLA Modules:
  0.0 79.2 jit_solution(3348967330057299458)
XLA Ops:
  0.6 74.0 %shard_map.59 = (f32[1024,512]{1,0:T(8,128)}, bf16[128,8192]{1,0:T(8,128)(2,1)}) custom-call(bf16[128,8192]{1,0:T(8,128)(2,1)} %x_in.1, f32[1,8192]{1,0:T(1,128)} %bitcast.1, bf16[1024,512]{1,0:T(8,128)(2,1)} %w_in.1, bf16[128,512]{1,0:T(8,128)(2,1)} %dy_in.1), custom_call_target="tpu_custom_call" | custom-call | tf_op jit(solution)/shard_map/pallas_call | solution.py:333
  74.7 0.0 copy-start
  74.7 3.2 %copy.8 = f32[1024,512]{1,0:T(8,128)} copy(f32[1024,512]{1,0:T(8,128)} %get-tuple-element.4) | data formatting | bytes 4194304
  77.9 0.0 copy-done
  77.9 1.3 %copy.9 = bf16[128,8192]{1,0:T(8,128)(2,1)} copy(bf16[128,8192]{1,0:T(8,128)(2,1)S(1)} %copy-done) | data formatting | bytes 4194304
Async XLA Ops:
  74.7 3.2 %copy-start = (bf16[128,8192]{1,0:T(8,128)(2,1)S(1)}, bf16[128,8192]{1,0:T(8,128)(2,1)}, u32[]{:S(2)}) copy-start(bf16[128,8192]{1,0:T(8,128)(2,1)} %get-tuple-element.5) | copy-start | bytes 6291460

commit v6 on v3

--- a/solution.py
+++ b/solution.py
@@ -252,9 +252,9 @@
     def send_rows(k):
         fin[peer(k)] = finish(peer(k))
         o_copy(k).start()
-    loop(1, S, send_rows)
     out[rows(g), fcols(s, c)] = finish(s)
     send_on(0)
+    loop(1, S, send_rows)
 
     def mate_block(k):
         sec = source(k)

time: 78.9 us -> 79.1 us (level)
  no operation moved by 1% of the time
where the time goes in v6:
time: 79.1 us; the launch traced here: 78.9 us
  Pallas kernels  73.7 us (93%)
  local copies, waits for them, and re-layouts  4.55 us (6%)
    pallas_call x1, Pallas kernels, per_device(): pl.pallas_call(functools.partial(kernel, S, T), out_shape=(jax.ShapeDtype...  73.7 us
    unnamed x4, local copies, waits for them, and re-layouts  4.55 us

profile of v6, /device:TPU:1, one launch (start us, length us, event | category | flops | bytes accessed | tf_op | source)
XLA Modules:
  0.0 78.9 jit_solution(3769165040437354345)
XLA Ops:
  0.6 73.7 %shard_map.59 = (f32[1024,512]{1,0:T(8,128)}, bf16[128,8192]{1,0:T(8,128)(2,1)}) custom-call(bf16[128,8192]{1,0:T(8,128)(2,1)} %x.1, f32[1,8192]{1,0:T(1,128)} %bitcast.1, bf16[1024,512]{1,0:T(8,128)(2,1)} %w.1, bf16[128,512]{1,0:T(8,128)(2,1)} %dyin.1), custom_call_target="tpu_custom_call" | custom-call | tf_op jit(solution)/shard_map/pallas_call | solution.py:335
  74.4 0.0 copy-start
  74.4 3.2 %copy.8 = f32[1024,512]{1,0:T(8,128)} copy(f32[1024,512]{1,0:T(8,128)} %get-tuple-element.4) | data formatting | bytes 4194304
  77.6 0.0 copy-done
  77.6 1.3 %copy.9 = bf16[128,8192]{1,0:T(8,128)(2,1)} copy(bf16[128,8192]{1,0:T(8,128)(2,1)S(1)} %copy-done) | data formatting | bytes 4194304
Async XLA Ops:
  74.4 3.2 %copy-start = (bf16[128,8192]{1,0:T(8,128)(2,1)S(1)}, bf16[128,8192]{1,0:T(8,128)(2,1)}, u32[]{:S(2)}) copy-start(bf16[128,8192]{1,0:T(8,128)(2,1)} %get-tuple-element.5) | copy-start | bytes 6291460
